TPU v7x, 32 devices: a whole 2x2x4 slice. The times are simulated.
32 devices in a mesh: row: 8 (over y, x, core), col: 4 (over z).
Axes of the slice: x: 2, y: 2, z: 4, core: 2. Of those that a mesh axis runs over, the one named last changes fastest.
Arguments:
- amplitudes: bfloat16 [4096, 4096], P('row', 'col'), may hold values from -0.1875 to 0.1875
- factors: bfloat16 [4096, 2048], P('col', 'row'), may hold values from -0.125 to 0.125
- tile_map: int32 [16, 16], P('row', 'col'), may hold values 0 or 1
- panel_owner: int32 [2], replicated, may hold values from 0 to 3, as said below
Outputs:
- cycle_term: float32 [4096, 4096], P('row', 'col')
Inputs may be any that keep to these rules, and one draw needn't show every extreme that they name: `panel_owner`: the 2 entries are distinct panel indices, and one of them is the last panel.
All inputs are finite; a program needn't handle non-finite values. No bound on the sum of `tile_map` on one device may be relied on, other than what follows from the above.
Results may differ from a plain program's by a relative error of at most 0.0029.
Values may be sent and summed in bfloat16 or wider, within the bound.
A program may use at most 64 MiB of HBM per device.

v0:
```python
import jax
import jax.numpy as jnp
from jax import lax
from jax.sharding import PartitionSpec as P


def spread(block, axis, owner):
    block = jnp.where(lax.axis_index(axis) == owner, block, jnp.zeros_like(block))
    return lax.psum(block, axis)


def keep_tiles(block, tiles):
    rows, cols = tiles.shape
    shaped = block.reshape(rows, block.shape[0] // rows, cols, block.shape[1] // cols)
    keep = tiles.astype(block.dtype)[:, None, :, None]
    return (shaped * keep).reshape(block.shape)


def outer_rows(left, right):
    return lax.dot_general(
        left, right, (((1,), (1,)), ((), ())), preferred_element_type=jnp.float32
    )


def shards(amplitudes, factors, tile_map, panel_owner):
    kept = keep_tiles(amplitudes, tile_map)
    width = factors.shape[0]
    total = jnp.zeros((kept.shape[0], width), jnp.float32)
    column_factors = lax.all_gather(factors, "row", axis=1, tiled=True)
    for step in range(panel_owner.shape[0]):
        owner = panel_owner[step]
        panel = spread(kept, "col", owner)
        owner_slice = spread(factors, "col", owner)
        owner_factors = lax.all_gather(owner_slice, "row", axis=1, tiled=True)
        integrals = outer_rows(owner_factors, column_factors).astype(jnp.bfloat16)
        total = total + jnp.dot(panel, integrals, preferred_element_type=jnp.float32)
    return keep_tiles(total, tile_map)


def solution(mesh):
    in_specs = (P("row", "col"), P("col", "row"), P("row", "col"), P())
    out_specs = P("row", "col")
    return jax.shard_map(shards, mesh=mesh, in_specs=in_specs, out_specs=out_specs, check_vma=False)
```

profile of v0, /device:TPU:0, one launch (start us, length us, event | category | flops | bytes accessed | tf_op | source)
XLA Modules:
  0.0 232.9 jit_solution(12405336362898462879)
XLA Ops:
  7.4 0.0 all-reduce.3.cloned.1.call-start
  7.4 0.8 fusion.10
  8.2 1.3 fusion.11
  9.4 0.3 mul.22
  9.8 0.2 copy.5
  11.2 2.1 broadcast_select_fusion.3
  13.3 0.0 copy-done
  13.3 1.5 broadcast_select_fusion.1
  14.8 0.0 all-reduce.3.cloned.1.call-update
  14.9 0.0 all-gather.6.cloned.1.call-start
  14.9 0.5 all-gather.6.cloned.1.call-update
  15.4 0.0 all-gather.8.cloned.1.call-start
  15.5 123.3 %all-reduce.3.cloned.1.call-done = (bf16[512,1024]{1,0:T(8,128)(2,1)}, bf16[1024,256]{1,0:T(8,128)(2,1)}, bf16[512,1024]{1,0:T(8,128)(2,1)}, bf16[1024,256]{1,0:T(8,128)(2,1)}) async-done(((bf16[512,1024]{1,0:T(8,128)(2,1)}, bf16[1024,256]{1,0:T(8,128)(2,1)}, bf16[512,1024]{1,0:T(8,128)(2,1)}, bf16[1024,256]{1,0:T(8,128)(2,1)}), (bf16[512,1024]{1,0:T(8,128)(2,1)}, bf16[1024,256]{1,0:T(8,128)(2,1)}, ...) | async-done | bytes 3145744 | tf_op jit(solution)/shard_map/psum | solution.py:9
  138.8 0.0 all-gather.8.cloned.1.call-update
  138.9 0.0 all-gather.4.cloned.1.call-start
  138.9 0.5 all-gather.4.cloned.1.call-update
  139.4 0.3 mul.25
  139.8 0.5 copy.6
  140.3 0.0 all-gather.6.cloned.1.call-done
  140.3 34.9 %all-gather.8.cloned.1.call-done = bf16[1024,2048]{1,0:T(8,128)(2,1)} async-done(((bf16[1024,256]{1,0:T(8,128)(2,1)}), bf16[1024,2048]{1,0:T(8,128)(2,1)}) %all-gather.8.cloned.1.call-update) | async-done | bytes 4194320 | tf_op jit(solution)/shard_map/all_gather | solution.py:34
  175.2 10.8 %fusion = f32[512,1024]{1,0:T(8,128)} fusion(bf16[512,1024]{1,0:T(8,128)(2,1)} %get-tuple-element.5, bf16[1024,2048]{1,0:T(8,128)(2,1)} %all-gather.8.cloned.1.call-done, bf16[1024,2048]{1,0:T(8,128)(2,1)} %all-gather.6.cloned.1.call-done), kind=kOutput, calls=%fused_computation.1 | convolution fusion | flops 5369757696 | bytes 11534336 | tf_op jit(solution)/shard_map/dot_general | solution.py:36
  186.0 28.2 %all-gather.4.cloned.1.call-done = bf16[1024,2048]{1,0:T(8,128)(2,1)} async-done(((bf16[1024,256]{1,0:T(8,128)(2,1)}), bf16[1024,2048]{1,0:T(8,128)(2,1)}) %all-gather.4.cloned.1.call-update) | async-done | bytes 4194320 | tf_op jit(solution)/shard_map/all_gather | solution.py:34
  214.2 0.0 copy-done.1
  214.2 11.1 %add_multiply_fusion = f32[512,1024]{1,0:T(8,128)} fusion(f32[512,1024]{1,0:T(8,128)S(1)} %bitcast.17, f32[512,1024]{1,0:T(8,128)} %fusion, bf16[512,1024]{1,0:T(8,128)(2,1)S(1)} %copy-done.1, bf16[1024,2048]{1,0:T(8,128)(2,1)} %all-gather.4.cloned.1.call-done, bf16[1024,2048]{1,0:T(8,128)(2,1)} %all-gather.6.cloned.1.call-done), kind=kOutput, calls=%fused_computation | convolution fusion | flops 5370806272 | bytes 15728640 | tf_op jit(solution)/shard_map/dot_general | solution.py:36
  (2 shorter events, 0.0 us)
Async XLA Ops:
  7.4 6.0 %copy-start = (bf16[512,1024]{1,0:T(8,128)(2,1)S(1)}, bf16[512,1024]{1,0:T(8,128)(2,1)}, u32[]{:S(2)}) copy-start(bf16[512,1024]{1,0:T(8,128)(2,1)} %param.4) | copy-start | bytes 3145732
  7.4 131.5 %all-reduce.3.cloned.1.call-start = ((), (), s32[]{:S(2)}) async-start(), calls=%async_computation.3 | async-start | bytes 6291456 | tf_op jit(solution)/shard_map/psum | solution.py:9
  14.9 125.4 %all-gather.6.cloned.1.call-start = ((), (), s32[]{:S(2)}) async-start(), calls=%async_computation.1 | async-start | bytes 4718592 | tf_op jit(solution)/shard_map/all_gather | solution.py:29
  15.4 159.8 %all-gather.8.cloned.1.call-start = ((), (), s32[]{:S(2)}) async-start(), calls=%async_computation.2 | async-start | bytes 4718592 | tf_op jit(solution)/shard_map/all_gather | solution.py:34
  138.9 75.3 %all-gather.4.cloned.1.call-start = ((), (), s32[]{:S(2)}) async-start(), calls=%async_computation | async-start | bytes 4718592 | tf_op jit(solution)/shard_map/all_gather | solution.py:34
  175.2 39.0 %copy-start.1 = (bf16[512,1024]{1,0:T(8,128)(2,1)S(1)}, bf16[512,1024]{1,0:T(8,128)(2,1)}, u32[]{:S(2)}) copy-start(bf16[512,1024]{1,0:T(8,128)(2,1)} %get-tuple-element.7) | copy-start | bytes 3145732
Sparse Core Ops, SparseCore 0:
  15.0 123.8 all-reduce.2
Sparse Core Ops, SparseCore 1:
  17.2 39.9 all-gather.5
  139.0 36.2 all-gather.7
  177.0 37.2 all-gather.3
where the time goes:
time: 233 us
  waiting for transfers between devices  188 us (81%)
  matrix products  21.9 us (9%)
  between operations  16.3 us (7%)
  other arithmetic  4.41 us (2%)
  local copies, waits for them, and re-layouts  2.65 us (1%)
    psum x1, waiting for transfers between devices, spread(): return lax.psum(block, axis)  123 us
    all_gather x2, waiting for transfers between devices, shards(): owner_factors = lax.all_gather(owner_slice, 'row', axis=1, tiled=True)  63.1 us
    dot_general x2, matrix products, shards(): jnp.dot(panel, integrals, preferred_element_type=jnp.float32)  21.9 us
  transfers between devices with their start and end apart: 4, of which 3 were waited for; matrix products, arithmetic and copies ran while one was open for 5% of the time, Pallas kernels for 0%

commit v1 on v0

--- a/solution.py
+++ b/solution.py
@@ -6,7 +6,7 @@
 
 def spread(block, axis, owner):
     block = jnp.where(lax.axis_index(axis) == owner, block, jnp.zeros_like(block))
-    return lax.psum(block, axis)
+    return jnp.sum(lax.all_gather(block, axis), axis=0)
 
 
 def keep_tiles(block, tiles):

time: 233 us -> 402 us (1.73)
  waiting for transfers between devices: 188 us -> 344 us
  other arithmetic: 4.41 us -> 17.8 us
    all_gather x0 -> x4, waiting for transfers between devices: none -> 241 us  [spread(): return jnp.sum(lax.all_gather(block, axis), axis=0)]
    psum x1 -> x0, waiting for transfers between devices: 123 us -> none  [spread(): return lax.psum(block, axis)]
    all_gather x1, waiting for transfers between devices: 0.03 us -> 34.3 us  [shards(): column_factors = lax.all_gather(factors, 'row', axis=1, tiled=True)]
    reduce_sum x0 -> x4, other arithmetic: none -> 13.4 us  [spread(): return jnp.sum(lax.all_gather(block, axis), axis=0)]
    all_gather x2, waiting for transfers between devices: 63.1 us -> 67.6 us  [shards(): owner_factors = lax.all_gather(owner_slice, 'row', axis=1, tiled=True)]
  transfers between devices with their start and end apart: 4 -> 7, of which waited for: 3 -> 7; matrix products, arithmetic and copies ran while one was open for 5% -> 7% of each run, Pallas kernels for 0% -> 0%
where the time goes in v1:
time: 402 us
  waiting for transfers between devices  344 us (86%)
  matrix products  21.7 us (5%)
  other arithmetic  17.8 us (4%)
  between operations  14.8 us (4%)
    all_gather x4, waiting for transfers between devices, spread(): return jnp.sum(lax.all_gather(block, axis), axis=0)  241 us
    all_gather x2, waiting for transfers between devices, shards(): owner_factors = lax.all_gather(owner_slice, 'row', axis=1, tiled=True)  67.6 us
    all_gather x1, waiting for transfers between devices, shards(): column_factors = lax.all_gather(factors, 'row', axis=1, tiled=True)  34.3 us
    dot_general x2, matrix products, shards(): jnp.dot(panel, integrals, preferred_element_type=jnp.float32)  21.7 us
    reduce_sum x4, other arithmetic, spread(): return jnp.sum(lax.all_gather(block, axis), axis=0)  13.4 us
  transfers between devices with their start and end apart: 7, of which 7 were waited for; matrix products, arithmetic and copies ran while one was open for 7% of the time, Pallas kernels for 0%

profile of v1, /device:TPU:0, one launch (start us, length us, event | category | flops | bytes accessed | tf_op | source)
XLA Modules:
  0.0 401.6 jit_solution(3979388865257668337)
XLA Ops:
  6.5 1.4 fusion.11
  9.2 2.1 broadcast_select_fusion.3
  11.4 0.7 all-gather.20.cloned.1.call-update
  12.2 0.8 fusion.10
  12.9 0.3 mul.22
  13.3 0.2 copy.5
  13.5 1.5 broadcast_select_fusion.1
  15.1 0.5 all-gather.18.cloned.1.call-update
  15.6 0.5 all-gather.14.cloned.1.call-update
  16.2 43.7 %all-gather.24.cloned.1.call-done = bf16[4096,256]{1,0:T(8,128)(2,1)} async-done(((bf16[1024,256]{1,0:T(8,128)(2,1)}), bf16[4096,256]{1,0:T(8,128)(2,1)}) %all-gather.24.cloned.1.call-update) | async-done | bytes 2097168 | tf_op jit(solution)/shard_map/all_gather | solution.py:9
  59.9 2.8 reduce_sum.51
  62.8 43.1 %all-gather.20.cloned.1.call-done = bf16[4096,256]{1,0:T(8,128)(2,1)} async-done(((bf16[1024,256]{1,0:T(8,128)(2,1)}), bf16[4096,256]{1,0:T(8,128)(2,1)}) %all-gather.20.cloned.1.call-update) | async-done | bytes 2097168 | tf_op jit(solution)/shard_map/all_gather | solution.py:9
  106.0 2.9 reduce_sum.49
  108.9 0.3 mul.25
  109.2 0.5 copy.6
  109.7 77.4 %all-gather.22.cloned.1.call-done = bf16[2048,1024]{1,0:T(8,128)(2,1)} async-done(((bf16[512,1024]{1,0:T(8,128)(2,1)}), bf16[2048,1024]{1,0:T(8,128)(2,1)}) %all-gather.22.cloned.1.call-update) | async-done | bytes 4194320 | tf_op jit(solution)/shard_map/all_gather | solution.py:9
  187.1 4.4 %reduce_sum.50 = bf16[512,1024]{1,0:T(8,128)(2,1)} reduce(bf16[4,512,1024]{2,1,0:T(8,128)(2,1)} %bitcast.20, bf16[]{:T(256)} %constant.11.clone.1), dimensions={0}, to_apply=%region_2.3 | reduce | flops 1572864 | bytes 5242882 | tf_op jit(solution)/shard_map/reduce_sum | solution.py:9
  191.5 76.3 %all-gather.18.cloned.1.call-done = bf16[2048,1024]{1,0:T(8,128)(2,1)} async-done(((bf16[512,1024]{1,0:T(8,128)(2,1)}), bf16[2048,1024]{1,0:T(8,128)(2,1)}) %all-gather.18.cloned.1.call-update) | async-done | bytes 4194320 | tf_op jit(solution)/shard_map/all_gather | solution.py:9
  267.8 3.3 reduce_sum.48
  271.1 34.3 %all-gather.14.cloned.1.call-done = bf16[1024,2048]{1,0:T(8,128)(2,1)} async-done(((bf16[1024,256]{1,0:T(8,128)(2,1)}), bf16[1024,2048]{1,0:T(8,128)(2,1)}) %all-gather.14.cloned.1.call-update) | async-done | bytes 4194320 | tf_op jit(solution)/shard_map/all_gather | solution.py:29
  305.4 39.1 %all-gather.16.cloned.1.call-done = bf16[1024,2048]{1,0:T(8,128)(2,1)} async-done(((bf16[1024,256]{1,0:T(8,128)(2,1)}), bf16[1024,2048]{1,0:T(8,128)(2,1)}) %all-gather.16.cloned.1.call-update) | async-done | bytes 4194320 | tf_op jit(solution)/shard_map/all_gather | solution.py:34
  344.5 10.7 %fusion = f32[512,1024]{1,0:T(8,128)} fusion(bf16[512,1024]{1,0:T(8,128)(2,1)} %reduce_sum.50, bf16[1024,2048]{1,0:T(8,128)(2,1)} %all-gather.16.cloned.1.call-done, bf16[1024,2048]{1,0:T(8,128)(2,1)} %all-gather.14.cloned.1.call-done), kind=kOutput, calls=%fused_computation.1 | convolution fusion | flops 5369757696 | bytes 11534336 | tf_op jit(solution)/shard_map/dot_general | solution.py:36
  355.2 28.5 %all-gather.12.cloned.1.call-done = bf16[1024,2048]{1,0:T(8,128)(2,1)} async-done(((bf16[1024,256]{1,0:T(8,128)(2,1)}), bf16[1024,2048]{1,0:T(8,128)(2,1)}) %all-gather.12.cloned.1.call-update) | async-done | bytes 4194320 | tf_op jit(solution)/shard_map/all_gather | solution.py:34
  383.7 11.0 %add_multiply_fusion = f32[512,1024]{1,0:T(8,128)} fusion(f32[512,1024]{1,0:T(8,128)S(1)} %bitcast.25, f32[512,1024]{1,0:T(8,128)} %fusion, bf16[512,1024]{1,0:T(8,128)(2,1)S(1)} %reduce_sum.48, bf16[1024,2048]{1,0:T(8,128)(2,1)} %all-gather.12.cloned.1.call-done, bf16[1024,2048]{1,0:T(8,128)(2,1)} %all-gather.14.cloned.1.call-done), kind=kOutput, calls=%fused_computation | convolution fusion | flops 5370806272 | bytes 15728640 | tf_op jit(solution)/shard_map/dot_general | solution.py:36
  (13 shorter events, 0.3 us)
Async XLA Ops:
  6.5 7.0 %copy-start = (bf16[512,1024]{1,0:T(8,128)(2,1)S(1)}, bf16[512,1024]{1,0:T(8,128)(2,1)}, u32[]{:S(2)}) copy-start(bf16[512,1024]{1,0:T(8,128)(2,1)} %param.4) | copy-start | bytes 3145732
  6.5 53.4 %all-gather.24.cloned.1.call-start = ((), (), s32[]{:S(2)}) async-start(), calls=%async_computation.6 | async-start | bytes 2621440 | tf_op jit(solution)/shard_map/all_gather | solution.py:9
  11.4 94.6 %all-gather.20.cloned.1.call-start = ((), (), s32[]{:S(2)}) async-start(), calls=%async_computation.4 | async-start | bytes 2621440 | tf_op jit(solution)/shard_map/all_gather | solution.py:9
  12.1 175.0 %all-gather.22.cloned.1.call-start = ((), (), s32[]{:S(2)}) async-start(), calls=%async_computation.5 | async-start | bytes 5242880 | tf_op jit(solution)/shard_map/all_gather | solution.py:9
  15.0 252.8 %all-gather.18.cloned.1.call-start = ((), (), s32[]{:S(2)}) async-start(), calls=%async_computation.3 | async-start | bytes 5242880 | tf_op jit(solution)/shard_map/all_gather | solution.py:9
  15.6 289.8 %all-gather.14.cloned.1.call-start = ((), (), s32[]{:S(2)}) async-start(), calls=%async_computation.1 | async-start | bytes 4718592 | tf_op jit(solution)/shard_map/all_gather | solution.py:29
  16.2 328.3 %all-gather.16.cloned.1.call-start = ((), (), s32[]{:S(2)}) async-start(), calls=%async_computation.2 | async-start | bytes 4718592 | tf_op jit(solution)/shard_map/all_gather | solution.py:34
  62.8 321.0 %all-gather.12.cloned.1.call-start = ((), (), s32[]{:S(2)}) async-start(), calls=%async_computation | async-start | bytes 4718592 | tf_op jit(solution)/shard_map/all_gather | solution.py:34
Sparse Core Ops, SparseCore 0:
  11.5 48.3 all-gather.23
  61.5 44.4 all-gather.19
  107.5 79.5 all-gather.21
  188.5 79.2 all-gather.17
  269.5 35.8 all-gather.13
  307.1 37.3 all-gather.15
  346.4 37.3 all-gather.11
